TPU v7x, 32 devices: a whole 2x2x4 slice. The times are simulated.
32 devices in a mesh: groups: 2 (over x), seq: 4 (over z), expert: 4 (over y, core).
Axes of the slice: x: 2, y: 2, z: 4, core: 2. Of those that a mesh axis runs over, the one named last changes fastest.
Arguments:
- q_lat: bfloat16 [512, 65536], P(('groups', 'seq'), 'expert'), parts along dimension 0, may hold values from -36 to 36
- q_rope: bfloat16 [512, 8192], P(('groups', 'seq'), 'expert'), parts along dimension 0, may hold values from -6 to 6
- cache_lat: bfloat16 [2048, 512], P(('groups', 'seq')), parts along dimension 0, may hold values from -7 to 7
- cache_rope: bfloat16 [2048, 64], P(('groups', 'seq')), parts along dimension 0, may hold values from -8 to 8
- tool_lat: bfloat16 [256, 512], P(('groups', 'seq')), parts along dimension 0, may hold values from -2.5 to 2.5
- tool_rope: bfloat16 [256, 64], P(('groups', 'seq')), parts along dimension 0, may hold values from -8 to 8
- offset: int32 [2], P('groups'), parts along dimension 0, may hold values from 512 to 736
- suf_lat: bfloat16 [512, 512], P(('groups', 'seq')), parts along dimension 0, may hold values from -6 to 6
- suf_rope: bfloat16 [512, 64], P(('groups', 'seq')), parts along dimension 0, may hold values from -8 to 8
- w_uv: bfloat16 [128, 512, 128], P('expert'), may hold values from -1 to 1
- w_out: bfloat16 [16384, 7168], P('expert', 'seq'), may hold values from -0.19921875 to 0.19921875
- resid: bfloat16 [512, 7168], P(('groups', 'expert'), 'seq'), parts along dimension 0, may hold values from -36 to 36
- routes: int32 [512, 2], P(('groups', 'expert')), parts along dimension 0, may hold values from 0 to 3, all different within a row; in each aligned block of 64 rows (0 to 63, 64 to 127, ...) at most 40 rows name the same one
- probs: float32 [512, 2], P(('groups', 'expert')), parts along dimension 0, may hold values from 0.1 to 1
- w_gate: bfloat16 [4, 7168, 1024], P('expert', None, 'seq'), may hold values from -0.0625 to 0.0625
- w_up: bfloat16 [4, 7168, 1024], P('expert', None, 'seq'), may hold values from -0.0625 to 0.0625
- w_down: bfloat16 [4, 1024, 7168], P('expert', 'seq'), may hold values from -0.1875 to 0.1875
Outputs:
- attn_residual: bfloat16 [512, 7168], P(('groups', 'expert'), 'seq'), parts along dimension 0
- expert_mix: bfloat16 [512, 7168], P(('groups', 'expert'), 'seq'), parts along dimension 0
There are 2 independent parts, one for each index of `groups`. A program takes and returns all parts, laid end to end along the dimension named above; an argument that names none is the same for every part. Nothing has to cross between parts.
Inputs may be any that keep to these rules, and one draw needn't show every extreme that they name: `routes`: within the rows of one device of the expert axis (64 rows in a row), no expert is named more than 40 times.
All inputs are finite; a program needn't handle non-finite values.
Results may differ from a plain program's by a relative error of at most 0.03.
Values may be sent and summed in bfloat16 or wider, within the bound.
No kernel may reach another device: no remote copies, remote signals or barrier semaphores. Data moves between devices by JAX's collectives and lax.ppermute only.
A program may use at most 128 MiB of HBM per device.

v0:
```python
import jax
import jax.numpy as jnp
from jax import lax
from jax.sharding import PartitionSpec as P

score_scale = 192.0 ** (-0.5)
floor_score = -1e30
norm_eps = 1e-06


def run_expert(tokens_in, w_gate, w_up, w_down):
    sources, count, width = tokens_in.shape
    rows = tokens_in.reshape(sources * count, width)
    gate = jnp.dot(rows, w_gate[0], preferred_element_type=jnp.float32)
    upper = jnp.dot(rows, w_up[0], preferred_element_type=jnp.float32)
    inner = (jax.nn.silu(gate) * upper).astype(jnp.bfloat16)
    partial_out = jnp.dot(inner, w_down[0], preferred_element_type=jnp.float32).reshape(
        sources, count, width
    )
    summed = lax.psum_scatter(
        partial_out.astype(jnp.bfloat16), "seq", scatter_dimension=2, tiled=True
    )
    return lax.all_to_all(summed, "expert", split_axis=0, concat_axis=0, tiled=True)


def on_device(
    q_lat,
    q_rope,
    cache_lat,
    cache_rope,
    tool_lat,
    tool_rope,
    offset,
    suf_lat,
    suf_rope,
    w_uv,
    w_out,
    resid,
    routes,
    probs,
    w_gate,
    w_up,
    w_down,
):
    seq_index = lax.axis_index("seq")
    ctx_dev = cache_lat.shape[0]
    query_dev = q_lat.shape[0]
    heads_dev, lat_width, value_width = w_uv.shape
    rope_width = cache_rope.shape[1]
    tool_all_lat, tool_all_rope = (
        lax.all_gather(tool_lat, "seq", axis=0, tiled=True),
        lax.all_gather(tool_rope, "seq", axis=0, tiled=True),
    )
    tool_len = tool_all_lat.shape[0]
    position = seq_index * ctx_dev + jnp.arange(ctx_dev, dtype=jnp.int32)
    shifted = position - offset[0]
    inside = (shifted >= 0) & (shifted < tool_len)
    safe = jnp.clip(shifted, 0, tool_len - 1)
    ctx_lat = jnp.where(inside[:, None], jnp.take(tool_all_lat, safe, axis=0), cache_lat)
    ctx_rope = jnp.where(inside[:, None], jnp.take(tool_all_rope, safe, axis=0), cache_rope)
    local_lat = jnp.concatenate([ctx_lat, suf_lat], axis=0)
    local_rope = jnp.concatenate([ctx_rope, suf_rope], axis=0)
    block_len = ctx_dev + query_dev
    query_rows = query_dev * heads_dev
    queries_lat = q_lat.reshape(query_rows, lat_width)
    queries_rope = q_rope.reshape(query_rows, rope_width)
    query_pos = seq_index * query_dev + jnp.arange(query_rows, dtype=jnp.int32) // heads_dev
    running_max = jnp.full((query_rows,), floor_score, jnp.float32)
    piece_lat = lax.all_gather(local_lat, "seq", axis=0, tiled=True)
    piece_rope = lax.all_gather(local_rope, "seq", axis=0, tiled=True)
    global_row = jnp.arange(piece_lat.shape[0], dtype=jnp.int32)
    within = global_row % block_len
    owner = global_row // block_len
    is_context = within < ctx_dev
    suffix_pos = owner * query_dev + within - ctx_dev
    visible = is_context[None, :] | (suffix_pos[None, :] <= query_pos[:, None])
    scores = jnp.einsum("qc,kc->qk", queries_lat, piece_lat, preferred_element_type=jnp.float32)
    scores = (
        scores
        + jnp.einsum("qc,kc->qk", queries_rope, piece_rope, preferred_element_type=jnp.float32)
    ) * score_scale
    scores = jnp.where(visible, scores, floor_score)
    new_max = jnp.maximum(running_max, jnp.max(scores, axis=1))
    weights = jnp.where(visible, jnp.exp(scores - new_max[:, None]), 0.0)
    new_total = jnp.sum(weights, axis=1)
    new_acc = jnp.dot(weights.astype(jnp.bfloat16), piece_lat, preferred_element_type=jnp.float32)
    latent_out = (
        (new_acc / new_total[:, None]).astype(jnp.bfloat16).reshape(query_dev, heads_dev, lat_width)
    )
    head_vals = jnp.einsum(
        "thc,hcv->thv", latent_out, w_uv, preferred_element_type=jnp.float32
    ).astype(jnp.bfloat16)
    head_vals = head_vals.reshape(query_dev, heads_dev * value_width)
    all_values = lax.all_gather(head_vals, "seq", axis=0, tiled=True)
    tok_dev = resid.shape[0]
    attn_sum = lax.psum_scatter(
        jnp.dot(all_values, w_out, preferred_element_type=jnp.float32).astype(jnp.bfloat16),
        "expert",
        scatter_dimension=0,
        tiled=True,
    ).astype(jnp.float32)
    attn_residual = (resid.astype(jnp.float32) + attn_sum).astype(jnp.bfloat16)
    expert_count = lax.axis_size("expert") * w_gate.shape[0]
    top_count = routes.shape[1]
    capacity = tok_dev * top_count * 5 // (4 * expert_count)
    flat_routes = routes.reshape(-1)
    one_hot = (flat_routes[:, None] == jnp.arange(expert_count, dtype=jnp.int32)[None, :]).astype(
        jnp.int32
    )
    earlier = jnp.cumsum(one_hot, axis=0) - one_hot
    slot = jnp.sum(earlier * one_hot, axis=1)
    target = (flat_routes * capacity + slot).reshape(tok_dev, top_count)
    slot_ids = jnp.arange(expert_count * capacity, dtype=jnp.int32)
    matches = slot_ids[:, None, None] == target[None, :, :]
    send_matrix = jnp.any(matches, axis=2).astype(jnp.bfloat16)
    route_weight = 2.5 * probs / jnp.sum(probs, axis=1, keepdims=True)
    gather_matrix = jnp.sum(jnp.where(matches, route_weight[None, :, :], 0.0), axis=2).T
    whole_stream = lax.all_gather(attn_residual, "seq", axis=1, tiled=True).astype(jnp.float32)
    normed = (
        whole_stream
        * lax.rsqrt(jnp.mean(whole_stream * whole_stream, axis=1, keepdims=True) + norm_eps)
    ).astype(jnp.bfloat16)
    outgoing = jnp.dot(send_matrix, normed, preferred_element_type=jnp.float32).astype(jnp.bfloat16)
    outgoing = outgoing.reshape(expert_count, capacity, normed.shape[1])
    returned = run_expert(
        lax.all_to_all(outgoing, "expert", split_axis=0, concat_axis=0, tiled=True),
        w_gate,
        w_up,
        w_down,
    )
    returned = returned.reshape(expert_count * capacity, returned.shape[2]).astype(jnp.float32)
    expert_mix = jnp.dot(
        gather_matrix, returned, precision=lax.Precision.HIGHEST, preferred_element_type=jnp.float32
    )
    return (attn_residual, expert_mix.astype(jnp.bfloat16))


def solution(mesh):
    placed = (
        P(("groups", "seq"), "expert"),
        P(("groups", "seq"), "expert"),
        P(("groups", "seq"), None),
        P(("groups", "seq"), None),
        P(("groups", "seq"), None),
        P(("groups", "seq"), None),
        P("groups"),
        P(("groups", "seq"), None),
        P(("groups", "seq"), None),
        P("expert", None, None),
        P("expert", "seq"),
        P(("groups", "expert"), "seq"),
        P(("groups", "expert"), None),
        P(("groups", "expert"), None),
        P("expert", None, "seq"),
        P("expert", None, "seq"),
        P("expert", "seq", None),
    )
    return jax.shard_map(
        on_device,
        mesh=mesh,
        in_specs=placed,
        out_specs=(P(("groups", "expert"), "seq"), P(("groups", "expert"), "seq")),
        check_vma=False,
    )
```

profile of v0, /device:TPU:0, one launch (start us, length us, event | category | flops | bytes accessed | tf_op | source)
XLA Modules:
  0.0 289.8 jit_solution(17597389861939251030)
XLA Ops:
  8.1 15.3 %all_gather.18 = bf16[128,512]{1,0:T(8,128)(2,1)S(1)} all-gather(bf16[32,512]{1,0:T(8,128)(2,1)} %param.21), channel_id=1, replica_groups=mesh['groups'=2,'seq'=4,'expert'=4] {'seq'}, dimensions={0}, use_global_device_ids=true | all-gather | bytes 163840 | tf_op jit(solution)/shard_map/all_gather | solution.py:51
  23.4 1.2 gather_fusion
  24.5 1.1 select_select_fusion
  25.7 1.6 pad_maximum_fusion
  27.4 2.4 reshape.119
  29.7 13.2 %all_gather.20 = bf16[128,64]{1,0:T(8,128)(2,1)S(1)} all-gather(bf16[32,64]{1,0:T(8,128)(2,1)S(1)} %copy-done.8), channel_id=1, replica_groups=mesh['groups'=2,'seq'=4,'expert'=4] {'seq'}, dimensions={0}, use_global_device_ids=true | all-gather | bytes 20480 | tf_op jit(solution)/shard_map/all_gather | solution.py:52
  43.0 0.9 gather_fusion.1
  44.3 15.6 %all-gather = bf16[4,320,64]{1,2,0:T(8,128)(2,1)S(1)} all-gather(bf16[1,320,64]{1,2,0:T(8,128)(2,1)S(1)} %copy.59), channel_id=1, replica_groups=mesh['groups'=2,'seq'=4,'expert'=4] {'seq'}, dimensions={0}, use_global_device_ids=true | all-gather | bytes 204800 | tf_op jit(solution)/shard_map/all_gather | solution.py:70
  60.2 0.5 reshape.120
  60.8 3.9 %all-gather.4.cloned.1.call-done = bf16[1280,512]{1,0:T(8,128)(2,1)} async-done(((bf16[320,512]{1,0:T(8,128)(2,1)}), bf16[1280,512]{1,0:T(8,128)(2,1)}) %all-gather.4.cloned.1.call-update) | async-done | bytes 1310736 | tf_op jit(solution)/shard_map/all_gather | solution.py:69
  64.7 5.0 %fusion.51 = f32[1280,2048]{1,0:T(8,128)S(1)} fusion(bf16[1280,512]{1,0:T(8,128)(2,1)} %all-gather.4.cloned.1.call-done, bf16[2048,512]{1,0:T(8,128)(2,1)} %reshape.119), kind=kOutput, calls=%fused_computation.80 | convolution fusion | flops 2684354560 | bytes 13893632 | tf_op jit(solution)/shard_map/qc,kc->qk/dot_general | solution.py:77
  69.6 4.1 %fusion.50 = (f32[2048]{0:T(1024)S(1)}, f32[2048,1280]{0,1:T(8,128)S(1)}) fusion(f32[1280,2048]{1,0:T(8,128)S(1)} %fusion.51, bf16[1280,64]{0,1:T(8,128)(2,1)S(1)} %reshape.143, bf16[2048,64]{1,0:T(8,128)(2,1)S(1)} %reshape.120, s32[2048]{0:T(1024)S(1)} %fusion.40, s32[1280]{0:T(1024)S(1)} %fusion.38, pred[1280]{0:T(1024)(128)(4,1)S(1)} %fusion.45), kind=kOutput, calls=%fused_computation.79 | convolution fusion | flops 351270912 | bytes 21420288 | tf_op jit(solution)/shard_map/qc,kc->qk/dot_general | solution.py:80
  73.7 3.9 %fusion = f32[2048]{0:T(1024)S(1)} fusion(f32[2048,1280]{0,1:T(8,128)S(1)} %get-tuple-element.3, f32[2048]{0:T(1024)S(1)} %broadcast_maximum_fusion, s32[2048]{0:T(1024)S(1)} %fusion.40, s32[1280]{0:T(1024)S(1)} %fusion.38, pred[1280]{0:T(1024)(128)(4,1)S(1)} %fusion.45), kind=kLoop, calls=%fused_computation.7 | loop fusion | flops 13105152 | bytes 10516736 | tf_op jit(solution)/shard_map/reduce_sum | solution.py:85
  77.7 4.5 %divide_convert_fusion = bf16[2048,512]{1,0:T(8,128)(2,1)S(1)} fusion(f32[2048]{0:T(1024)S(1)} %fusion, bf16[1280,512]{1,0:T(8,128)(2,1)S(1)} %copy-done.13, f32[2048,1280]{0,1:T(8,128)S(1)} %get-tuple-element.3, f32[2048]{0:T(1024)S(1)} %broadcast_maximum_fusion, s32[2048]{0:T(1024)S(1)} %fusion.40, s32[1280]{0:T(1024)S(1)} %fusion.38, ...), kind=kOutput, calls=%fused_computation.15 | convolution fusion | flops 2699558912 | bytes 13924608 | tf_op jit(solution)/shard_map/dot_general | solution.py:86
  82.3 2.5 fusion.23
  84.8 0.9 copy.73
  85.8 44.8 %all-gather.6.cloned.1.call-done = bf16[256,4096]{1,0:T(8,128)(2,1)} async-done(((bf16[64,4096]{1,0:T(8,128)(2,1)}), bf16[256,4096]{1,0:T(8,128)(2,1)}) %all-gather.6.cloned.1.call-update) | async-done | bytes 2097168 | tf_op jit(solution)/shard_map/all_gather | solution.py:94
  130.6 10.7 %convolution_convert_fusion.2 = bf16[256,1792]{1,0:T(8,128)(2,1)} fusion(bf16[256,4096]{1,0:T(8,128)(2,1)} %all-gather.6.cloned.1.call-done, bf16[4096,1792]{1,0:T(8,128)(2,1)} %param.27), kind=kOutput, calls=%fused_computation.21 | convolution fusion | flops 3758555136 | bytes 17694720 | tf_op jit(solution)/shard_map/dot_general | solution.py:97
  142.7 21.6 %reduce-scatter.3.cloned.1.call-done = bf16[64,1792]{1,0:T(8,128)(2,1)} async-done(((bf16[256,1792]{1,0:T(8,128)(2,1)}), bf16[64,1792]{1,0:T(8,128)(2,1)}) %reduce-scatter.3.cloned.1.call-update) | async-done | bytes 229392 | tf_op jit(solution)/shard_map/reduce_scatter | solution.py:96
  164.3 1.0 add_convert_fusion
  165.3 21.0 %all_gather.23 = bf16[64,7168]{1,0:T(8,128)(2,1)S(1)} all-gather(bf16[64,1792]{1,0:T(8,128)(2,1)S(1)} %add_convert_fusion), channel_id=1, replica_groups=mesh['groups'=2,'seq'=4,'expert'=4] {'seq'}, dimensions={1}, use_global_device_ids=true | all-gather | bytes 1146880 | tf_op jit(solution)/shard_map/all_gather | solution.py:118
  186.6 0.8 convolution_convert_fusion.1
  187.5 30.4 %all_to_all.10 = bf16[4,40,7168]{2,1,0:T(8,128)(2,1)S(1)} all-to-all(bf16[4,40,7168]{2,1,0:T(8,128)(2,1)S(1)} %bitcast.51), channel_id=1, replica_groups=mesh['groups'=2,'seq'=4,'expert'=4] {'expert'}, dimensions={0} | all-to-all | bytes 4587520 | tf_op jit(solution)/shard_map/all_to_all | solution.py:126
  217.8 0.8 fusion.12
  218.6 1.3 copy-done.11
  219.9 0.8 fusion.29
  220.7 1.3 copy-done.12
  221.9 2.2 convolution_convert_fusion
  224.1 45.3 %reduce-scatter.5.cloned.1.call-done = bf16[4,40,1792]{2,1,0:T(8,128)(2,1)} async-done(((bf16[4,40,7168]{2,1,0:T(8,128)(2,1)}), bf16[4,40,1792]{2,1,0:T(8,128)(2,1)}) %reduce-scatter.5.cloned.1.call-update) | async-done | bytes 573456 | tf_op jit(solution)/shard_map/reduce_scatter | solution.py:20
  269.4 3.5 %all-to-all-start.1 = ((bf16[4,40,1792]{2,1,0:T(8,128)(2,1)}), bf16[4,40,1792]{2,1,0:T(8,128)(2,1)S(1)}, u32[]{:S(2)}, u32[]{:S(2)}) async-start(bf16[4,40,1792]{2,1,0:T(8,128)(2,1)} %reduce-scatter.5.cloned.1.call-done), calls=%async_computation.3 | async-start | bytes 1146880 | tf_op jit(solution)/shard_map/all_to_all | solution.py:23
  273.1 9.2 %all-to-all-done.1 = bf16[4,40,1792]{2,1,0:T(8,128)(2,1)S(1)} async-done(((bf16[4,40,1792]{2,1,0:T(8,128)(2,1)}), bf16[4,40,1792]{2,1,0:T(8,128)(2,1)S(1)}, u32[]{:S(2)}, u32[]{:S(2)}) %all-to-all-start.1) | async-done | bytes 573472 | tf_op jit(solution)/shard_map/all_to_all | solution.py:23
  282.2 1.1 convolution_convert_fusion.3
  (61 shorter events, 2.7 us)
Async XLA Ops:
  7.2 20.2 %copy-start.2 = (bf16[64,16384]{1,0:T(8,128)(2,1)S(1)}, bf16[64,16384]{1,0:T(8,128)(2,1)}, u32[]{:S(2)}) copy-start(bf16[64,16384]{1,0:T(8,128)(2,1)} %param.17) | copy-start | bytes 6291460
  7.2 57.5 %all-gather.4.cloned.1.call-start = ((), (), s32[]{:S(2)}) async-start(), calls=%async_computation.4 | async-start | bytes 1638400 | tf_op jit(solution)/shard_map/all_gather | solution.py:69
  23.4 6.4 %copy-start.8 = (bf16[32,64]{1,0:T(8,128)(2,1)S(1)}, bf16[32,64]{1,0:T(8,128)(2,1)}, u32[]{:S(2)}) copy-start(bf16[32,64]{1,0:T(8,128)(2,1)} %param.22) | copy-start | bytes 12292
  24.5 19.3 %copy-start.6 = (bf16[256,64]{0,1:T(8,128)(2,1)S(1)}, bf16[256,64]{0,1:T(8,128)(2,1)}, u32[]{:S(2)}) copy-start(bf16[256,64]{0,1:T(8,128)(2,1)} %param.20) | copy-start | bytes 98308
  24.5 19.6 %copy-start.7 = (bf16[64,64]{1,0:T(8,128)(2,1)S(1)}, bf16[64,64]{1,0:T(8,128)(2,1)}, u32[]{:S(2)}) copy-start(bf16[64,64]{1,0:T(8,128)(2,1)} %param.25) | copy-start | bytes 24580
  25.6 34.5 %copy-start.4 = (bf16[64,2048]{1,0:T(8,128)(2,1)S(1)}, bf16[64,2048]{1,0:T(8,128)(2,1)}, u32[]{:S(2)}) copy-start(bf16[64,2048]{1,0:T(8,128)(2,1)} %param.18) | copy-start | bytes 786436
  27.3 103.3 %all-gather.6.cloned.1.call-start = ((), (), s32[]{:S(2)}) async-start(), calls=%async_computation.5 | async-start | bytes 2621440 | tf_op jit(solution)/shard_map/all_gather | solution.py:94
  73.7 4.0 %copy-start.13 = (bf16[1280,512]{1,0:T(8,128)(2,1)S(1)}, bf16[1280,512]{1,0:T(8,128)(2,1)}, u32[]{:S(2)}) copy-start(bf16[1280,512]{1,0:T(8,128)(2,1)} %all-gather.4.cloned.1.call-done) | copy-start | bytes 3932164
  77.7 4.6 %copy-start = (bf16[32,512,128]{2,1,0:T(8,128)(2,1)S(1)}, bf16[32,512,128]{2,1,0:T(8,128)(2,1)}, u32[]{:S(2)}) copy-start(bf16[32,512,128]{2,1,0:T(8,128)(2,1)} %param.26) | copy-start | bytes 12582916
  85.7 55.9 %copy-start.9 = (s32[64,2]{0,1:T(2,128)S(1)}, s32[64,2]{0,1:T(2,128)}, u32[]{:S(2)}) copy-start(s32[64,2]{0,1:T(2,128)} %param.29) | copy-start | bytes 1540
  85.7 78.6 %copy-start.5 = (bf16[64,1792]{1,0:T(8,128)(2,1)S(1)}, bf16[64,1792]{1,0:T(8,128)(2,1)}, u32[]{:S(2)}) copy-start(bf16[64,1792]{1,0:T(8,128)(2,1)} %param.28) | copy-start | bytes 688132
  85.7 78.6 %reduce-scatter.3.cloned.1.call-start = ((), (), s32[]{:S(2)}) async-start(), calls=%async_computation.6 | async-start | bytes 1146880 | tf_op jit(solution)/shard_map/reduce_scatter | solution.py:96
  141.4 128.1 %reduce-scatter.5.cloned.1.call-start = ((), (), s32[]{:S(2)}) async-start(), calls=%async_computation.7 | async-start | bytes 2867200 | tf_op jit(solution)/shard_map/reduce_scatter | solution.py:20
  165.3 52.5 %copy-start.3 = (bf16[64,1792]{1,0:T(8,128)(2,1)}, bf16[64,1792]{1,0:T(8,128)(2,1)S(1)}, u32[]{:S(2)}) copy-start(bf16[64,1792]{1,0:T(8,128)(2,1)S(1)} %add_convert_fusion) | copy-start | bytes 688132
  186.6 31.2 %copy-start.1 = (bf16[1,7168,256]{2,1,0:T(8,128)(2,1)S(1)}, bf16[1,7168,256]{2,1,0:T(8,128)(2,1)}, u32[]{:S(2)}) copy-start(bf16[1,7168,256]{2,1,0:T(8,128)(2,1)} %param.31) | copy-start | bytes 11010052
  217.8 2.0 copy-start.11
  219.9 2.0 copy-start.12
  221.9 51.0 %copy-start.10 = (f32[64,2]{0,1:T(2,128)S(1)}, f32[64,2]{0,1:T(2,128)}, u32[]{:S(2)}) copy-start(f32[64,2]{0,1:T(2,128)} %param.30) | copy-start | bytes 1540
  269.4 12.8 %all-to-all-start.1 = ((bf16[4,40,1792]{2,1,0:T(8,128)(2,1)}), bf16[4,40,1792]{2,1,0:T(8,128)(2,1)S(1)}, u32[]{:S(2)}, u32[]{:S(2)}) async-start(bf16[4,40,1792]{2,1,0:T(8,128)(2,1)} %reduce-scatter.5.cloned.1.call-done), calls=%async_computation.3 | async-start | bytes 1146880 | tf_op jit(solution)/shard_map/all_to_all | solution.py:23
Sparse Core Ops, SparseCore 0:
  27.4 37.1 all-gather.3
  85.8 44.7 all-gather.5
  141.5 22.7 reduce-scatter.2
  224.3 45.1 reduce-scatter.4
where the time goes:
time: 290 us
  waiting for transfers between devices  125 us (43%)
  blocking collectives  95.5 us (33%)
  matrix products  32.4 us (11%)
  between operations  14.9 us (5%)
  local copies, waits for them, and re-layouts  9.37 us (3%)
  other arithmetic  8.86 us (3%)
  starting transfers between devices  3.86 us (1%)
    reduce_scatter x1, waiting for transfers between devices, run_expert(): lax.psum_scatter(partial_out.astype(jnp.bfloat16), 'seq', scatter_dimensi...  45.3 us
    all_gather x1, waiting for transfers between devices, on_device(): all_values = lax.all_gather(head_vals, 'seq', axis=0, tiled=True)  44.8 us
    all_to_all x1, blocking collectives, on_device(): lax.all_to_all(outgoing, 'expert', split_axis=0, concat_axis=0, tiled=True)  30.4 us
    reduce_scatter x1, waiting for transfers between devices, on_device(): lax.psum_scatter(jnp.dot(all_values, w_out, preferred_element_type=jnp.fl...  21.6 us
    all_gather x1, blocking collectives, on_device(): lax.all_gather(attn_residual, 'seq', axis=1, tiled=True).astype(jnp.float32)  21 us
    all_gather x1, blocking collectives, on_device(): piece_rope = lax.all_gather(local_rope, 'seq', axis=0, tiled=True)  15.6 us
    all_gather x1, blocking collectives, on_device(): lax.all_gather(tool_lat, 'seq', axis=0, tiled=True)  15.3 us
    all_gather x1, blocking collectives, on_device(): lax.all_gather(tool_rope, 'seq', axis=0, tiled=True)  13.2 us
  transfers between devices with their start and end apart: 5, of which 5 were waited for; matrix products, arithmetic and copies ran while one was open for 2% of the time, Pallas kernels for 0%

commit v1 on v0

--- a/solution.py
+++ b/solution.py
@@ -66,8 +66,11 @@
     queries_rope = q_rope.reshape(query_rows, rope_width)
     query_pos = seq_index * query_dev + jnp.arange(query_rows, dtype=jnp.int32) // heads_dev
     running_max = jnp.full((query_rows,), floor_score, jnp.float32)
-    piece_lat = lax.all_gather(local_lat, "seq", axis=0, tiled=True)
-    piece_rope = lax.all_gather(local_rope, "seq", axis=0, tiled=True)
+    piece_lat, piece_rope = jnp.split(
+        lax.all_gather(jnp.concatenate([local_lat, local_rope], axis=1), "seq", axis=0, tiled=True),
+        [local_lat.shape[1]],
+        axis=1,
+    )
     global_row = jnp.arange(piece_lat.shape[0], dtype=jnp.int32)
     within = global_row % block_len
     owner = global_row // block_len

time: 290 us -> 306 us (1.055)
  waiting for transfers between devices: 125 us -> 158 us
  blocking collectives: 95.5 us -> 80.2 us
    all_gather x1, waiting for transfers between devices: 3.91 us -> 36.6 us  [on_device(): lax.all_gather(jnp.concatenate([local_lat, local_rope], axis=1), 'seq', a...]
    all_gather x1 -> x0, blocking collectives: 15.6 us -> none  [on_device(): piece_rope = lax.all_gather(local_rope, 'seq', axis=0, tiled=True)]
  transfers between devices with their start and end apart: 5 -> 5, of which waited for: 5 -> 5; matrix products, arithmetic and copies ran while one was open for 2% -> 1% of each run, Pallas kernels for 0% -> 0%
where the time goes in v1:
time: 306 us
  waiting for transfers between devices  158 us (52%)
  blocking collectives  80.2 us (26%)
  matrix products  31.6 us (10%)
  between operations  14.9 us (5%)
  local copies, waits for them, and re-layouts  9.72 us (3%)
  other arithmetic  7.99 us (3%)
  starting transfers between devices  3.64 us (1%)
    reduce_scatter x1, waiting for transfers between devices, run_expert(): lax.psum_scatter(partial_out.astype(jnp.bfloat16), 'seq', scatter_dimensi...  45.3 us
    all_gather x1, waiting for transfers between devices, on_device(): all_values = lax.all_gather(head_vals, 'seq', axis=0, tiled=True)  44.6 us
    all_gather x1, waiting for transfers between devices, on_device(): lax.all_gather(jnp.concatenate([local_lat, local_rope], axis=1), 'seq', a...  36.6 us
    all_to_all x1, blocking collectives, on_device(): lax.all_to_all(outgoing, 'expert', split_axis=0, concat_axis=0, tiled=True)  30.6 us
    reduce_scatter x1, waiting for transfers between devices, on_device(): lax.psum_scatter(jnp.dot(all_values, w_out, preferred_element_type=jnp.fl...  21.9 us
    all_gather x1, blocking collectives, on_device(): lax.all_gather(attn_residual, 'seq', axis=1, tiled=True).astype(jnp.float32)  21 us
    all_gather x1, blocking collectives, on_device(): lax.all_gather(tool_lat, 'seq', axis=0, tiled=True)  15.3 us
    all_gather x1, blocking collectives, on_device(): lax.all_gather(tool_rope, 'seq', axis=0, tiled=True)  13.3 us
  transfers between devices with their start and end apart: 5, of which 5 were waited for; matrix products, arithmetic and copies ran while one was open for 1% of the time, Pallas kernels for 0%

profile of v1, /device:TPU:0, one launch (start us, length us, event | category | flops | bytes accessed | tf_op | source)
XLA Modules:
  0.0 305.7 jit_solution(8582636202565000320)
XLA Ops:
  8.1 15.3 %all_gather.15 = bf16[128,512]{1,0:T(8,128)(2,1)S(1)} all-gather(bf16[32,512]{1,0:T(8,128)(2,1)} %param.21), channel_id=1, replica_groups=mesh['groups'=2,'seq'=4,'expert'=4] {'seq'}, dimensions={0}, use_global_device_ids=true | all-gather | bytes 163840 | tf_op jit(solution)/shard_map/all_gather | solution.py:51
  23.4 13.3 %all_gather.16 = bf16[128,64]{1,0:T(8,128)(2,1)S(1)} all-gather(bf16[32,64]{1,0:T(8,128)(2,1)} %param.22), channel_id=1, replica_groups=mesh['groups'=2,'seq'=4,'expert'=4] {'seq'}, dimensions={0}, use_global_device_ids=true | all-gather | bytes 20480 | tf_op jit(solution)/shard_map/all_gather | solution.py:52
  36.7 1.2 gather_fusion
  37.9 0.9 gather_fusion.1
  38.7 0.9 copy.39
  39.6 1.1 select_select_fusion
  40.9 0.8 maximum_maximum_fusion
  41.8 2.4 reshape.119
  44.1 0.5 reshape.120
  44.7 36.6 %all-gather.3.cloned.1.call-done = bf16[1280,576]{1,0:T(8,128)(2,1)} async-done(((bf16[320,576]{1,0:T(8,128)(2,1)}), bf16[1280,576]{1,0:T(8,128)(2,1)}) %all-gather.3.cloned.1.call-update) | async-done | bytes 1474576 | tf_op jit(solution)/shard_map/all_gather | solution.py:70
  81.3 5.1 %fusion.27 = f32[1280,2048]{1,0:T(8,128)S(1)} fusion(bf16[2048,512]{1,0:T(8,128)(2,1)} %reshape.119, bf16[1280,576]{1,0:T(8,128)(2,1)} %all-gather.3.cloned.1.call-done), kind=kOutput, calls=%fused_computation.32 | convolution fusion | flops 2684354560 | bytes 13893632 | tf_op jit(solution)/shard_map/qc,kc->qk/dot_general | solution.py:80
  86.4 3.2 %fusion.54 = (f32[2048]{0:T(1024)S(1)}, f32[2048,1280]{0,1:T(8,128)S(1)}) fusion(f32[1280,2048]{1,0:T(8,128)S(1)} %fusion.27, bf16[2048,64]{1,0:T(8,128)(2,1)S(1)} %reshape.120, bf16[1280,576]{1,0:T(8,128)(2,1)S(1)} %copy-done.7, s32[2048]{0:T(1024)S(1)} %fusion.44, s32[1280]{0:T(1024)S(1)} %fusion.42, pred[1280]{0:T(1024)(128)(4,1)S(1)} %fusion.49), kind=kOutput, calls=%fused_computation.82 | convolution fusion | flops 351270912 | bytes 21850112 | tf_op jit(solution)/shard_map/qc,kc->qk/dot_general | solution.py:83
  89.6 3.9 %fusion = f32[2048]{0:T(1024)S(1)} fusion(f32[2048,1280]{0,1:T(8,128)S(1)} %get-tuple-element.3, f32[2048]{0:T(1024)S(1)} %broadcast_maximum_fusion, s32[2048]{0:T(1024)S(1)} %fusion.44, s32[1280]{0:T(1024)S(1)} %fusion.42, pred[1280]{0:T(1024)(128)(4,1)S(1)} %fusion.49), kind=kLoop, calls=%fused_computation.7 | loop fusion | flops 13105152 | bytes 10516736 | tf_op jit(solution)/shard_map/reduce_sum | solution.py:88
  93.6 4.5 %divide_convert_fusion = bf16[2048,512]{1,0:T(8,128)(2,1)S(1)} fusion(f32[2048]{0:T(1024)S(1)} %fusion, f32[2048,1280]{0,1:T(8,128)S(1)} %get-tuple-element.3, f32[2048]{0:T(1024)S(1)} %broadcast_maximum_fusion, s32[2048]{0:T(1024)S(1)} %fusion.44, s32[1280]{0:T(1024)S(1)} %fusion.42, pred[1280]{0:T(1024)(128)(4,1)S(1)} %fusion.49, ...), kind=kOutput, calls=%fused_computation.15 | convolution fusion | flops 2699558912 | bytes 13928448 | tf_op jit(solution)/shard_map/dot_general | solution.py:89
  98.1 2.5 fusion.23
  100.7 0.9 copy.52
  101.7 44.6 %all-gather.5.cloned.1.call-done = bf16[256,4096]{1,0:T(8,128)(2,1)} async-done(((bf16[64,4096]{1,0:T(8,128)(2,1)}), bf16[256,4096]{1,0:T(8,128)(2,1)}) %all-gather.5.cloned.1.call-update) | async-done | bytes 2097168 | tf_op jit(solution)/shard_map/all_gather | solution.py:97
  146.2 10.7 %convolution_convert_fusion.2 = bf16[256,1792]{1,0:T(8,128)(2,1)} fusion(bf16[256,4096]{1,0:T(8,128)(2,1)} %all-gather.5.cloned.1.call-done, bf16[4096,1792]{1,0:T(8,128)(2,1)} %param.27), kind=kOutput, calls=%fused_computation.21 | convolution fusion | flops 3758555136 | bytes 17694720 | tf_op jit(solution)/shard_map/dot_general | solution.py:100
  158.0 21.9 %reduce-scatter.3.cloned.1.call-done = bf16[64,1792]{1,0:T(8,128)(2,1)} async-done(((bf16[256,1792]{1,0:T(8,128)(2,1)}), bf16[64,1792]{1,0:T(8,128)(2,1)}) %reduce-scatter.3.cloned.1.call-update) | async-done | bytes 229392 | tf_op jit(solution)/shard_map/reduce_scatter | solution.py:99
  180.0 1.0 add_convert_fusion
  181.0 21.0 %all_gather.19 = bf16[64,7168]{1,0:T(8,128)(2,1)S(1)} all-gather(bf16[64,1792]{1,0:T(8,128)(2,1)S(1)} %add_convert_fusion), channel_id=1, replica_groups=mesh['groups'=2,'seq'=4,'expert'=4] {'seq'}, dimensions={1}, use_global_device_ids=true | all-gather | bytes 1146880 | tf_op jit(solution)/shard_map/all_gather | solution.py:121
  202.3 0.8 convolution_convert_fusion.1
  203.1 30.6 %all_to_all.10 = bf16[4,40,7168]{2,1,0:T(8,128)(2,1)S(1)} all-to-all(bf16[4,40,7168]{2,1,0:T(8,128)(2,1)S(1)} %bitcast.44), channel_id=1, replica_groups=mesh['groups'=2,'seq'=4,'expert'=4] {'expert'}, dimensions={0} | all-to-all | bytes 4587520 | tf_op jit(solution)/shard_map/all_to_all | solution.py:129
  233.7 0.8 fusion.12
  234.5 1.3 copy-done.11
  235.7 0.8 fusion.32
  236.5 1.3 copy-done.12
  237.8 2.2 convolution_convert_fusion
  240.0 45.3 %reduce-scatter.5.cloned.1.call-done = bf16[4,40,1792]{2,1,0:T(8,128)(2,1)} async-done(((bf16[4,40,7168]{2,1,0:T(8,128)(2,1)}), bf16[4,40,1792]{2,1,0:T(8,128)(2,1)}) %reduce-scatter.5.cloned.1.call-update) | async-done | bytes 573456 | tf_op jit(solution)/shard_map/reduce_scatter | solution.py:20
  285.3 3.5 %all-to-all-start.1 = ((bf16[4,40,1792]{2,1,0:T(8,128)(2,1)}), bf16[4,40,1792]{2,1,0:T(8,128)(2,1)S(1)}, u32[]{:S(2)}, u32[]{:S(2)}) async-start(bf16[4,40,1792]{2,1,0:T(8,128)(2,1)} %reduce-scatter.5.cloned.1.call-done), calls=%async_computation.3 | async-start | bytes 1146880 | tf_op jit(solution)/shard_map/all_to_all | solution.py:23
  288.9 9.2 %all-to-all-done.1 = bf16[4,40,1792]{2,1,0:T(8,128)(2,1)S(1)} async-done(((bf16[4,40,1792]{2,1,0:T(8,128)(2,1)}), bf16[4,40,1792]{2,1,0:T(8,128)(2,1)S(1)}, u32[]{:S(2)}, u32[]{:S(2)}) %all-to-all-start.1) | async-done | bytes 573472 | tf_op jit(solution)/shard_map/all_to_all | solution.py:23
  298.0 1.1 convolution_convert_fusion.3
  (54 shorter events, 1.9 us)
Async XLA Ops:
  7.2 33.7 %copy-start.6 = (bf16[64,512]{1,0:T(8,128)(2,1)S(1)}, bf16[64,512]{1,0:T(8,128)(2,1)}, u32[]{:S(2)}) copy-start(bf16[64,512]{1,0:T(8,128)(2,1)} %param.24) | copy-start | bytes 196612
  7.2 33.7 %copy-start.8 = (bf16[64,64]{1,0:T(8,128)(2,1)S(1)}, bf16[64,64]{1,0:T(8,128)(2,1)}, u32[]{:S(2)}) copy-start(bf16[64,64]{1,0:T(8,128)(2,1)} %param.25) | copy-start | bytes 24580
  7.2 34.6 %copy-start.2 = (bf16[64,16384]{1,0:T(8,128)(2,1)S(1)}, bf16[64,16384]{1,0:T(8,128)(2,1)}, u32[]{:S(2)}) copy-start(bf16[64,16384]{1,0:T(8,128)(2,1)} %param.17) | copy-start | bytes 6291460
  7.2 74.1 %all-gather.3.cloned.1.call-start = ((), (), s32[]{:S(2)}) async-start(), calls=%async_computation.4 | async-start | bytes 2048000 | tf_op jit(solution)/shard_map/all_gather | solution.py:70
  37.9 6.3 %copy-start.4 = (bf16[64,2048]{1,0:T(8,128)(2,1)S(1)}, bf16[64,2048]{1,0:T(8,128)(2,1)}, u32[]{:S(2)}) copy-start(bf16[64,2048]{1,0:T(8,128)(2,1)} %param.18) | copy-start | bytes 786436
  41.7 104.5 %all-gather.5.cloned.1.call-start = ((), (), s32[]{:S(2)}) async-start(), calls=%async_computation.5 | async-start | bytes 2621440 | tf_op jit(solution)/shard_map/all_gather | solution.py:97
  81.3 5.1 %copy-start.7 = (bf16[1280,576]{1,0:T(8,128)(2,1)S(1)}, bf16[1280,576]{1,0:T(8,128)(2,1)}, u32[]{:S(2)}) copy-start(bf16[1280,576]{1,0:T(8,128)(2,1)} %all-gather.3.cloned.1.call-done) | copy-start | bytes 4423684
  93.6 4.5 %copy-start = (bf16[32,512,128]{2,1,0:T(8,128)(2,1)S(1)}, bf16[32,512,128]{2,1,0:T(8,128)(2,1)}, u32[]{:S(2)}) copy-start(bf16[32,512,128]{2,1,0:T(8,128)(2,1)} %param.26) | copy-start | bytes 12582916
  101.6 55.4 %copy-start.9 = (s32[64,2]{0,1:T(2,128)S(1)}, s32[64,2]{0,1:T(2,128)}, u32[]{:S(2)}) copy-start(s32[64,2]{0,1:T(2,128)} %param.29) | copy-start | bytes 1540
  101.6 78.4 %copy-start.5 = (bf16[64,1792]{1,0:T(8,128)(2,1)S(1)}, bf16[64,1792]{1,0:T(8,128)(2,1)}, u32[]{:S(2)}) copy-start(bf16[64,1792]{1,0:T(8,128)(2,1)} %param.28) | copy-start | bytes 688132
  101.6 78.3 %reduce-scatter.3.cloned.1.call-start = ((), (), s32[]{:S(2)}) async-start(), calls=%async_computation.6 | async-start | bytes 1146880 | tf_op jit(solution)/shard_map/reduce_scatter | solution.py:99
  157.0 128.3 %reduce-scatter.5.cloned.1.call-start = ((), (), s32[]{:S(2)}) async-start(), calls=%async_computation.7 | async-start | bytes 2867200 | tf_op jit(solution)/shard_map/reduce_scatter | solution.py:20
  181.0 52.7 %copy-start.3 = (bf16[64,1792]{1,0:T(8,128)(2,1)}, bf16[64,1792]{1,0:T(8,128)(2,1)S(1)}, u32[]{:S(2)}) copy-start(bf16[64,1792]{1,0:T(8,128)(2,1)S(1)} %add_convert_fusion) | copy-start | bytes 688132
  202.3 31.4 %copy-start.1 = (bf16[1,7168,256]{2,1,0:T(8,128)(2,1)S(1)}, bf16[1,7168,256]{2,1,0:T(8,128)(2,1)}, u32[]{:S(2)}) copy-start(bf16[1,7168,256]{2,1,0:T(8,128)(2,1)} %param.31) | copy-start | bytes 11010052
  233.7 2.0 copy-start.11
  235.7 2.0 copy-start.12
  237.8 51.0 %copy-start.10 = (f32[64,2]{0,1:T(2,128)S(1)}, f32[64,2]{0,1:T(2,128)}, u32[]{:S(2)}) copy-start(f32[64,2]{0,1:T(2,128)} %param.30) | copy-start | bytes 1540
  285.3 12.8 %all-to-all-start.1 = ((bf16[4,40,1792]{2,1,0:T(8,128)(2,1)}), bf16[4,40,1792]{2,1,0:T(8,128)(2,1)S(1)}, u32[]{:S(2)}, u32[]{:S(2)}) async-start(bf16[4,40,1792]{2,1,0:T(8,128)(2,1)} %reduce-scatter.5.cloned.1.call-done), calls=%async_computation.3 | async-start | bytes 1146880 | tf_op jit(solution)/shard_map/all_to_all | solution.py:23
Sparse Core Ops, SparseCore 0:
  41.8 39.4 all-gather.2
  101.7 44.4 all-gather.4
  157.1 22.8 reduce-scatter.2
  240.1 45.1 reduce-scatter.4
